TPU v7x, 512 devices: a whole 4x4x16 slice. The times are simulated.
512 devices in a mesh: grp: 4 (over z_hi, core), row: 4 (over x), col: 32 (over y, z_lo).
Axes of the slice: x: 4, y: 4, z: 16 (z_hi: 2, z_lo: 8; z = z_hi * 8 + z_lo), core: 2. Of those that a mesh axis runs over, the one named last changes fastest.
Arguments:
- acts: bfloat16 [768, 8192], P('grp', 'col'), may hold values from -6 to 6
- grads: bfloat16 [768, 28672], P('grp', ('row', 'col')), may hold values from -6 to 6
- basis_in: bfloat16 [8192, 4096], P('col', 'row'), may hold values from -0.0625 to 0.0625
- basis_out: bfloat16 [4, 7168, 14336], P('row', 'grp', 'col'), may hold values from -0.03125 to 0.03125
- lengths: int32 [4, 2], P('grp'), may hold values from 1 to 96, 144 in all within a row
Outputs:
- eigenvalues: float32 [14336, 4096], P('col', 'row')
Inputs may be any that keep to these rules, and one draw needn't show every extreme that they name: The 2 lengths of each index of grp sum to exactly 144, and none exceeds 96.
All inputs are finite; a program needn't handle non-finite values.
Results may differ from a plain program's by a relative error of at most 0.006.
Values may be sent and summed in bfloat16 or wider, within the bound.
No kernel may reach another device: no remote copies, remote signals or barrier semaphores. Data moves between devices by JAX's collectives and lax.ppermute only.
A program may use at most 64 MiB of HBM per device.

v0:
```python
import jax
import jax.numpy as jnp
from jax import lax
from jax.sharding import PartitionSpec as P

LEN = 96
VALID = 144


def rows_for(lines, size):
    spare = -len(lines) % size
    return jnp.pad(lines, [(0, spare)] + [(0, 0)] * (lines.ndim - 1))


def sum_by_parts(value, axis):
    lines = value.reshape(-1, *value.shape[1:][-1:])
    own = lax.psum_scatter(
        rows_for(lines, lax.axis_size(axis)), axis, scatter_dimension=0, tiled=True
    )
    whole = lax.all_gather(own, axis).reshape(-1, *lines.shape[1:])
    return lax.slice_in_dim(whole, 0, len(lines)).reshape(value.shape)


def outer_square(left, right):
    block = lax.dot_general(
        left, right, (((0,), (0,)), ((), ())), preferred_element_type=jnp.float32
    )
    return block * block


def per_device(acts, grads, basis_in, basis_out, lengths):
    seq_lens = lengths[0]
    count = seq_lens.shape[0]
    partial_in = jnp.dot(acts, basis_in, preferred_element_type=jnp.float32)
    proj_in = lax.psum(partial_in, "col").astype(jnp.bfloat16)
    ends = jnp.cumsum(seq_lens)
    starts = ends - seq_lens
    slot_ids = jnp.arange(VALID, dtype=jnp.int32)
    segment = jnp.sum((slot_ids[:, None] >= ends[None, :]).astype(jnp.int32), axis=1)
    member = segment[:, None] == jnp.arange(count, dtype=jnp.int32)[None, :]
    offset = jnp.sum(jnp.where(member, starts[None, :], 0), axis=1)
    source = segment * LEN + slot_ids - offset
    packed = jnp.take(grads, source, axis=0)
    gathered = lax.all_gather(packed, "col", axis=1, tiled=True)
    proj_in = jnp.take(proj_in, source, axis=0)
    partial_out = jnp.dot(
        gathered,
        lax.all_gather(basis_out, "grp", axis=1, tiled=True)[0],
        preferred_element_type=jnp.float32,
    )
    proj_out = lax.psum(partial_out, "row").astype(jnp.bfloat16)
    slot_pos = jnp.arange(LEN, dtype=jnp.int32)
    total = jnp.zeros((proj_out.shape[1], proj_in.shape[1]), jnp.float32)
    padded_out = jnp.concatenate(
        [proj_out, jnp.zeros((LEN, proj_out.shape[1]), jnp.bfloat16)], axis=0
    )
    padded_in = jnp.concatenate([proj_in, jnp.zeros((LEN, proj_in.shape[1]), jnp.bfloat16)], axis=0)
    for seq in range(count):
        keep = (slot_pos < seq_lens[seq]).astype(jnp.bfloat16)
        piece_out = lax.dynamic_slice_in_dim(padded_out, starts[seq], LEN, 0)
        piece_in = lax.dynamic_slice_in_dim(padded_in, starts[seq], LEN, 0)
        total = total + outer_square(piece_out * keep[:, None], piece_in)
    summed = sum_by_parts(total.astype(jnp.bfloat16), "grp").astype(jnp.float32)
    return summed / (lax.axis_size("grp") * count * LEN)


def solution(mesh):
    in_specs = (
        P("grp", "col"),
        P("grp", ("row", "col")),
        P("col", "row"),
        P("row", "grp", "col"),
        P("grp", None),
    )
    out_specs = P("col", "row")
    return jax.shard_map(
        per_device, mesh=mesh, in_specs=in_specs, out_specs=out_specs, check_vma=False
    )
```

profile of v0, /device:TPU:3, one launch (start us, length us, event | category | flops | bytes accessed | tf_op | source)
XLA Modules:
  0.0 542.7 jit_solution(12668688378372334434)
XLA Ops:
  6.5 0.0 copy-start
  6.5 0.9 reduce-window.4
  7.4 0.7 fusion.13
  8.1 0.1 fusion.9
  8.2 0.1 fusion.10
  8.3 1.7 gather_fusion
  10.0 0.7 select_bitcast_fusion
  10.7 0.0 all-gather.7.cloned.1.call-update
  10.8 0.0 all-gather.5.cloned.1.call-start
  10.8 0.7 all-gather.5.cloned.1.call-update
  11.5 0.0 reduce-scatter.2.cloned.1.call-start
  11.6 0.0 copy-done.2
  11.6 0.6 fusion.17
  14.6 0.3 fusion.18
  14.9 229.0 %all-reduce.5 = bf16[192,1024]{1,0:T(8,128)(2,1)S(1)} all-reduce(f32[192,1024]{1,0:T(8,128)S(1)} %fusion.18), channel_id=1, replica_groups=mesh['grp'=4,'row'=4,'col'=32] {'col'}, use_global_device_ids=true, to_apply=%region_4.5 | all-reduce | flops 196608 | bytes 1179648 | tf_op jit(solution)/shard_map/psum | solution.py:35
  243.9 0.9 gather_fusion.1
  246.0 0.6 fusion.16
  246.6 0.6 compare_convert_fusion.2
  247.1 0.6 compare_convert_fusion.1
  247.8 0.1 broadcast_select_fusion
  247.9 0.0 all-gather.7.cloned.1.call-done
  247.9 2.5 copy.8
  250.4 5.0 reshape.92
  255.4 150.0 %all-gather.5.cloned.1.call-done = bf16[1,7168,448]{1,2,0:T(8,128)(2,1)} async-done(((bf16[1,1792,448]{1,2,0:T(8,128)(2,1)}), bf16[1,7168,448]{1,2,0:T(8,128)(2,1)}) %all-gather.5.cloned.1.call-update) | async-done | bytes 6422544 | tf_op jit(solution)/shard_map/all_gather | solution.py:48
  405.4 5.5 %fusion = f32[144,448]{1,0:T(8,128)S(1)} fusion(bf16[7168,144]{0,1:T(8,128)(2,1)} %reshape.92, bf16[1,7168,448]{1,2,0:T(8,128)(2,1)} %all-gather.5.cloned.1.call-done), kind=kOutput, calls=%fused_computation.2 | convolution fusion | flops 924844032 | bytes 8744960 | tf_op jit(solution)/shard_map/dot_general | solution.py:46
  410.9 25.5 %all-reduce.4 = bf16[144,448]{1,0:T(8,128)(2,1)S(1)} all-reduce(f32[144,448]{1,0:T(8,128)S(1)} %fusion), channel_id=1, replica_groups=mesh['grp'=4,'row'=4,'col'=32] {'row'}, use_global_device_ids=true, to_apply=%region_3.4 | all-reduce | flops 64512 | bytes 387072 | tf_op jit(solution)/shard_map/psum | solution.py:51
  436.4 0.5 fusion.2
  436.9 1.4 add_convert_fusion
  438.3 0.0 reduce-scatter.2.cloned.1.call-update
  438.3 65.1 %reduce-scatter.2.cloned.1.call-done = bf16[112,1024]{1,0:T(8,128)(2,1)} async-done(((bf16[448,1024]{1,0:T(8,128)(2,1)}), bf16[112,1024]{1,0:T(8,128)(2,1)}) %reduce-scatter.2.cloned.1.call-update) | async-done | bytes 229392 | tf_op jit(solution)/shard_map/reduce_scatter | solution.py:17
  503.4 31.3 %all-gather = bf16[448,1024]{1,0:T(8,128)(2,1)S(1)} all-gather(bf16[112,1024]{1,0:T(8,128)(2,1)} %reduce-scatter.2.cloned.1.call-done), channel_id=2, replica_groups=mesh['grp'=4,'row'=4,'col'=32] {'grp'}, dimensions={0}, use_global_device_ids=true | all-gather | bytes 1146880 | tf_op jit(solution)/shard_map/all_gather | solution.py:20
  534.7 1.5 convert_multiply_fusion
  (10 shorter events, 0.0 us)
Async XLA Ops:
  6.5 8.0 %copy-start = (bf16[256,1024]{1,0:T(8,128)(2,1)S(1)}, bf16[256,1024]{1,0:T(8,128)(2,1)}, u32[]{:S(2)}) copy-start(bf16[256,1024]{1,0:T(8,128)(2,1)} %param.7) | copy-start | bytes 1572868
  6.5 5.0 copy-start.2
  6.5 8.1 %copy-start.1 = (bf16[192,256]{1,0:T(8,128)(2,1)S(1)}, bf16[192,256]{1,0:T(8,128)(2,1)}, u32[]{:S(2)}) copy-start(bf16[192,256]{1,0:T(8,128)(2,1)} %param.5) | copy-start | bytes 294916
  6.5 241.4 %all-gather.7.cloned.1.call-start = ((), (), s32[]{:S(2)}) async-start(), calls=%async_computation.3 | async-start | bytes 2433024 | tf_op jit(solution)/shard_map/all_gather | solution.py:44
  10.8 394.6 %all-gather.5.cloned.1.call-start = ((), (), s32[]{:S(2)}) async-start(), calls=%async_computation.1 | async-start | bytes 8028160 | tf_op jit(solution)/shard_map/all_gather | solution.py:48
  11.5 491.9 %reduce-scatter.2.cloned.1.call-start = ((), (), s32[]{:S(2)}) async-start(), calls=%async_computation.2 | async-start | bytes 1146880 | tf_op jit(solution)/shard_map/reduce_scatter | solution.py:17
Sparse Core Ops, SparseCore 0:
  10.9 215.8 all-gather.6
  228.9 176.4 all-gather.4
  438.5 64.9 reduce-scatter.1
where the time goes:
time: 543 us
  blocking collectives  286 us (53%)
  waiting for transfers between devices  216 us (40%)
  between operations  16.8 us (3%)
  local copies, waits for them, and re-layouts  11.3 us (2%)
  matrix products  7.65 us (1%)
    psum x1, blocking collectives, per_device(): proj_in = lax.psum(partial_in, 'col').astype(jnp.bfloat16)  229 us
    all_gather x1, waiting for transfers between devices, per_device(): lax.all_gather(basis_out, 'grp', axis=1, tiled=True)[0]  150 us
    reduce_scatter x1, waiting for transfers between devices, sum_by_parts(): lax.psum_scatter(rows_for(lines, lax.axis_size(axis)), axis, scatter_dime...  65.1 us
    all_gather x1, blocking collectives, sum_by_parts(): whole = lax.all_gather(own, axis).reshape(-1, *lines.shape[1:])  31.3 us
    psum x1, blocking collectives, per_device(): proj_out = lax.psum(partial_out, 'row').astype(jnp.bfloat16)  25.5 us
  transfers between devices with their start and end apart: 3, of which 2 were waited for; matrix products, arithmetic and copies ran while one was open for 2% of the time, Pallas kernels for 0%

commit v1 on v0

--- a/solution.py
+++ b/solution.py
@@ -45,7 +45,9 @@
     proj_in = jnp.take(proj_in, source, axis=0)
     partial_out = jnp.dot(
         gathered,
-        lax.all_gather(basis_out, "grp", axis=1, tiled=True)[0],
+        jnp.concatenate(
+            lax.all_to_all(jnp.stack([basis_out] * lax.axis_size("grp")), "grp", 0, 0), axis=1
+        )[0],
         preferred_element_type=jnp.float32,
     )
     proj_out = lax.psum(partial_out, "row").astype(jnp.bfloat16)

time: 543 us -> 735 us (1.35)
  blocking collectives: 286 us -> 569 us
  waiting for transfers between devices: 216 us -> 94.3 us
  local copies, waits for them, and re-layouts: 11.3 us -> 29.9 us
  starting transfers between devices: 0.08 us -> 15.9 us
    psum x1, blocking collectives: 229 us -> 520 us  [per_device(): proj_in = lax.psum(partial_in, 'col').astype(jnp.bfloat16)]
    all_gather x1 -> x0, waiting for transfers between devices: 150 us -> none  [per_device(): lax.all_gather(basis_out, 'grp', axis=1, tiled=True)[0]]
    reduce_scatter x1, waiting for transfers between devices: 65.1 us -> 94.2 us  [sum_by_parts(): lax.psum_scatter(rows_for(lines, lax.axis_size(axis)), axis, scatter_dime...]
    all_to_all x0 -> x1, starting transfers between devices: none -> 15.9 us  [per_device(): lax.all_to_all(jnp.stack([basis_out] * lax.axis_size('grp')), 'grp', 0, 0)]
    all_to_all x0 -> x1, local copies, waits for them, and re-layouts: none -> 10.5 us  [per_device(): lax.all_to_all(jnp.stack([basis_out] * lax.axis_size('grp')), 'grp', 0, 0)]
    psum x1, blocking collectives: 25.5 us -> 17 us  [per_device(): proj_out = lax.psum(partial_out, 'row').astype(jnp.bfloat16)]
  transfers between devices with their start and end apart: 3 -> 3, of which waited for: 2 -> 1; matrix products, arithmetic and copies ran while one was open for 2% -> 2% of each run, Pallas kernels for 0% -> 0%
where the time goes in v1:
time: 735 us; the launch traced here: 734 us
  blocking collectives  569 us (77%)
  waiting for transfers between devices  94.3 us (13%)
  local copies, waits for them, and re-layouts  29.9 us (4%)
  between operations  17.5 us (2%)
  starting transfers between devices  15.9 us (2%)
    psum x1, blocking collectives, per_device(): proj_in = lax.psum(partial_in, 'col').astype(jnp.bfloat16)  520 us
    reduce_scatter x1, waiting for transfers between devices, sum_by_parts(): lax.psum_scatter(rows_for(lines, lax.axis_size(axis)), axis, scatter_dime...  94.2 us
    all_gather x1, blocking collectives, sum_by_parts(): whole = lax.all_gather(own, axis).reshape(-1, *lines.shape[1:])  31.3 us
    psum x1, blocking collectives, per_device(): proj_out = lax.psum(partial_out, 'row').astype(jnp.bfloat16)  17 us
    all_to_all x1, starting transfers between devices, per_device(): lax.all_to_all(jnp.stack([basis_out] * lax.axis_size('grp')), 'grp', 0, 0)  15.9 us
  transfers between devices with their start and end apart: 3, of which 1 were waited for; matrix products, arithmetic and copies ran while one was open for 2% of the time, Pallas kernels for 0%

profile of v1, /device:TPU:3, one launch (start us, length us, event | category | flops | bytes accessed | tf_op | source)
XLA Modules:
  0.0 734.4 jit_solution(15074596825972032130)
XLA Ops:
  6.5 4.6 stack.2
  11.1 15.9 %all-to-all-start = ((bf16[4,1,1792,448]{2,3,1,0:T(8,128)(2,1)}), bf16[4,1,1792,448]{2,3,1,0:T(8,128)(2,1)}, u32[]{:S(2)}, u32[]{:S(2)}) async-start(bf16[4,1,1792,448]{2,3,1,0:T(8,128)(2,1)} %stack.2), calls=%async_computation | async-start | bytes 12845056 | tf_op jit(solution)/shard_map/all_to_all | solution.py:49
  27.0 0.2 reduce-window.4
  27.2 0.1 fusion.7
  27.3 0.1 fusion.8
  27.4 0.9 gather_fusion
  28.3 0.7 select_bitcast_fusion
  29.1 0.0 all-gather.4.cloned.1.call-update
  29.1 0.0 reduce-scatter.2.cloned.1.call-start
  29.1 0.6 fusion.15
  32.4 0.0 copy-done
  32.4 0.3 fusion.17
  32.7 520.3 %all-reduce.5 = bf16[192,1024]{1,0:T(8,128)(2,1)S(1)} all-reduce(f32[192,1024]{1,0:T(8,128)S(1)} %fusion.17), channel_id=1, replica_groups=mesh['grp'=4,'row'=4,'col'=32] {'col'}, use_global_device_ids=true, to_apply=%region_4.5 | all-reduce | flops 196608 | bytes 1179648 | tf_op jit(solution)/shard_map/psum | solution.py:35
  553.0 0.9 gather_fusion.1
  555.2 0.6 fusion.14
  555.9 0.7 compare_convert_fusion.2
  556.6 0.6 compare_convert_fusion.1
  557.2 0.1 broadcast_select_fusion
  557.3 0.0 all-gather.4.cloned.1.call-done
  557.4 2.5 copy.12
  559.8 4.9 reshape.95
  564.8 0.0 all-to-all-done
  564.8 10.5 %copy.13 = bf16[4,1,1792,448]{2,0,3,1:T(4,128)(2,1)} copy(bf16[4,1,1792,448]{2,3,1,0:T(8,128)(2,1)} %all-to-all-done) | data formatting | bytes 12845056 | tf_op jit(solution)/shard_map/all_to_all | solution.py:49
  575.2 4.3 copy.14
  579.6 2.0 fusion.16
  581.6 17.0 %all-reduce.4 = bf16[144,448]{1,0:T(8,128)(2,1)S(1)} all-reduce(f32[144,448]{1,0:T(8,128)S(1)} %fusion.16), channel_id=1, replica_groups=mesh['grp'=4,'row'=4,'col'=32] {'row'}, use_global_device_ids=true, to_apply=%region_3.4 | all-reduce | flops 64512 | bytes 387072 | tf_op jit(solution)/shard_map/psum | solution.py:53
  598.6 0.5 fusion
  599.1 1.4 add_convert_fusion
  600.5 0.0 reduce-scatter.2.cloned.1.call-update
  600.5 94.2 %reduce-scatter.2.cloned.1.call-done = bf16[112,1024]{1,0:T(8,128)(2,1)} async-done(((bf16[448,1024]{1,0:T(8,128)(2,1)}), bf16[112,1024]{1,0:T(8,128)(2,1)}) %reduce-scatter.2.cloned.1.call-update) | async-done | bytes 229392 | tf_op jit(solution)/shard_map/reduce_scatter | solution.py:17
  694.8 31.3 %all-gather = bf16[448,1024]{1,0:T(8,128)(2,1)S(1)} all-gather(bf16[112,1024]{1,0:T(8,128)(2,1)} %reduce-scatter.2.cloned.1.call-done), channel_id=2, replica_groups=mesh['grp'=4,'row'=4,'col'=32] {'grp'}, dimensions={0}, use_global_device_ids=true | all-gather | bytes 1146880 | tf_op jit(solution)/shard_map/all_gather | solution.py:20
  726.1 1.5 convert_multiply_fusion
  (16 shorter events, 0.1 us)
Async XLA Ops:
  6.5 25.9 %copy-start = (bf16[256,1024]{1,0:T(8,128)(2,1)S(1)}, bf16[256,1024]{1,0:T(8,128)(2,1)}, u32[]{:S(2)}) copy-start(bf16[256,1024]{1,0:T(8,128)(2,1)} %param.7) | copy-start | bytes 1572868
  11.1 15.9 %copy-start.4 = (s32[1,2]{1,0:T(1,128)S(1)}, s32[1,2]{1,0:T(1,128)}, u32[]{:S(2)}) copy-start(s32[1,2]{1,0:T(1,128)} %param.9) | copy-start | bytes 28
  11.1 16.3 %copy-start.2 = (bf16[192,224]{1,0:T(8,128)(2,1)S(1)}, bf16[192,224]{1,0:T(8,128)(2,1)}, u32[]{:S(2)}) copy-start(bf16[192,224]{1,0:T(8,128)(2,1)} %param.6) | copy-start | bytes 258052
  11.1 21.3 %copy-start.3 = (bf16[192,256]{1,0:T(8,128)(2,1)S(1)}, bf16[192,256]{1,0:T(8,128)(2,1)}, u32[]{:S(2)}) copy-start(bf16[192,256]{1,0:T(8,128)(2,1)} %param.5) | copy-start | bytes 294916
  11.1 553.6 %all-to-all-start = ((bf16[4,1,1792,448]{2,3,1,0:T(8,128)(2,1)}), bf16[4,1,1792,448]{2,3,1,0:T(8,128)(2,1)}, u32[]{:S(2)}, u32[]{:S(2)}) async-start(bf16[4,1,1792,448]{2,3,1,0:T(8,128)(2,1)} %stack.2), calls=%async_computation | async-start | bytes 12845056 | tf_op jit(solution)/shard_map/all_to_all | solution.py:49
  27.0 530.3 %all-gather.4.cloned.1.call-start = ((), (), s32[]{:S(2)}) async-start(), calls=%async_computation.3 | async-start | bytes 2433024 | tf_op jit(solution)/shard_map/all_gather | solution.py:44
  29.1 665.7 %reduce-scatter.2.cloned.1.call-start = ((), (), s32[]{:S(2)}) async-start(), calls=%async_computation.2 | async-start | bytes 1146880 | tf_op jit(solution)/shard_map/reduce_scatter | solution.py:17
  575.2 4.3 copy-start.1
Sparse Core Ops, SparseCore 0:
  29.9 362.1 all-gather.3
  600.7 94.0 reduce-scatter.1

commit v2 on v0

--- a/solution.py
+++ b/solution.py
@@ -32,7 +32,7 @@
     seq_lens = lengths[0]
     count = seq_lens.shape[0]
     partial_in = jnp.dot(acts, basis_in, preferred_element_type=jnp.float32)
-    proj_in = lax.psum(partial_in, "col").astype(jnp.bfloat16)
+    proj_in = jnp.sum(lax.all_gather(partial_in, "col"), axis=0).astype(jnp.bfloat16)
     ends = jnp.cumsum(seq_lens)
     starts = ends - seq_lens
     slot_ids = jnp.arange(VALID, dtype=jnp.int32)

time: 543 us -> 1080 us (1.99)
  waiting for transfers between devices: 216 us -> 976 us
  blocking collectives: 286 us -> 50.6 us
    all_gather x0 -> x1, waiting for transfers between devices: none -> 535 us  [per_device(): lax.all_gather(partial_in, 'col')]
    psum x1 -> x0, blocking collectives: 229 us -> none  [per_device(): proj_in = lax.psum(partial_in, 'col').astype(jnp.bfloat16)]
    all_gather x1, waiting for transfers between devices: 0.02 us -> 205 us  [per_device(): gathered = lax.all_gather(packed, 'col', axis=1, tiled=True)]
    all_gather x1, waiting for transfers between devices: 150 us -> 173 us  [per_device(): lax.all_gather(basis_out, 'grp', axis=1, tiled=True)[0]]
  transfers between devices with their start and end apart: 3 -> 4, of which waited for: 2 -> 4; matrix products, arithmetic and copies ran while one was open for 2% -> 2% of each run, Pallas kernels for 0% -> 0%
where the time goes in v2:
time: 1080 us
  waiting for transfers between devices  976 us (90%)
  blocking collectives  50.6 us (5%)
  between operations  17.2 us (2%)
  other arithmetic  14.5 us (1%)
  local copies, waits for them, and re-layouts  11.3 us (1%)
    all_gather x1, waiting for transfers between devices, per_device(): lax.all_gather(partial_in, 'col')  535 us
    all_gather x1, waiting for transfers between devices, per_device(): gathered = lax.all_gather(packed, 'col', axis=1, tiled=True)  205 us
    all_gather x1, waiting for transfers between devices, per_device(): lax.all_gather(basis_out, 'grp', axis=1, tiled=True)[0]  173 us
    reduce_scatter x1, waiting for transfers between devices, sum_by_parts(): lax.psum_scatter(rows_for(lines, lax.axis_size(axis)), axis, scatter_dime...  62.9 us
    all_gather x1, blocking collectives, sum_by_parts(): whole = lax.all_gather(own, axis).reshape(-1, *lines.shape[1:])  31.3 us
  transfers between devices with their start and end apart: 4, of which 4 were waited for; matrix products, arithmetic and copies ran while one was open for 2% of the time, Pallas kernels for 0%

profile of v2, /device:TPU:3, one launch (start us, length us, event | category | flops | bytes accessed | tf_op | source)
XLA Modules:
  0.0 1078.5 jit_solution(3196047604749573972)
XLA Ops:
  6.5 0.9 reduce-window.4
  7.4 0.7 fusion.13
  8.1 0.1 fusion.9
  8.2 0.1 fusion.10
  8.3 1.7 gather_fusion
  10.0 0.7 select_bitcast_fusion
  10.7 0.0 all-gather.11.cloned.1.call-update
  10.8 0.0 all-gather.7.cloned.1.call-start
  10.8 0.7 all-gather.7.cloned.1.call-update
  11.5 0.0 all-gather.9.cloned.1.call-start
  11.6 1.2 fusion.18
  12.7 0.0 all-gather.9.cloned.1.call-update
  12.8 0.0 reduce-scatter.2.cloned.1.call-start
  12.8 0.7 fusion.17
  17.4 0.7 fusion.16
  18.1 0.6 compare_convert_fusion.2
  18.7 0.7 compare_convert_fusion.1
  19.4 204.9 %all-gather.11.cloned.1.call-done = bf16[32,224,144]{1,2,0:T(8,128)(2,1)} async-done(((bf16[1,224,144]{1,2,0:T(8,128)(2,1)}), bf16[32,224,144]{1,2,0:T(8,128)(2,1)}) %all-gather.11.cloned.1.call-update) | async-done | bytes 2064400 | tf_op jit(solution)/shard_map/all_gather | solution.py:44
  224.3 2.5 copy.8
  226.8 4.9 reshape.93
  231.7 172.8 %all-gather.7.cloned.1.call-done = bf16[1,7168,448]{1,2,0:T(8,128)(2,1)} async-done(((bf16[1,1792,448]{1,2,0:T(8,128)(2,1)}), bf16[1,7168,448]{1,2,0:T(8,128)(2,1)}) %all-gather.7.cloned.1.call-update) | async-done | bytes 6422544 | tf_op jit(solution)/shard_map/all_gather | solution.py:48
  404.5 5.5 fusion
  410.0 19.4 %all-reduce.3 = bf16[144,448]{1,0:T(8,128)(2,1)S(1)} all-reduce(f32[144,448]{1,0:T(8,128)S(1)} %fusion), channel_id=1, replica_groups=mesh['grp'=4,'row'=4,'col'=32] {'row'}, use_global_device_ids=true, to_apply=%region_3.4 | all-reduce | flops 64512 | bytes 387072 | tf_op jit(solution)/shard_map/psum | solution.py:51
  429.4 534.8 %all-gather.9.cloned.1.call-done = f32[6144,1024]{1,0:T(8,128)} async-done(((f32[192,1024]{1,0:T(8,128)}), f32[6144,1024]{1,0:T(8,128)}) %all-gather.9.cloned.1.call-update) | async-done | bytes 25165840 | tf_op jit(solution)/shard_map/all_gather | solution.py:35
  964.2 9.2 reduce_sum.32
  973.3 0.9 gather_fusion.1
  974.3 0.1 broadcast_select_fusion
  974.4 0.5 fusion.2
  974.9 1.4 add_convert_fusion
  976.3 62.9 %reduce-scatter.2.cloned.1.call-done = bf16[112,1024]{1,0:T(8,128)(2,1)} async-done(((bf16[448,1024]{1,0:T(8,128)(2,1)}), bf16[112,1024]{1,0:T(8,128)(2,1)}) %reduce-scatter.2.cloned.1.call-update) | async-done | bytes 229392 | tf_op jit(solution)/shard_map/reduce_scatter | solution.py:17
  1039.2 31.3 %all-gather.1 = bf16[448,1024]{1,0:T(8,128)(2,1)S(1)} all-gather(bf16[112,1024]{1,0:T(8,128)(2,1)} %reduce-scatter.2.cloned.1.call-done), channel_id=3, replica_groups=mesh['grp'=4,'row'=4,'col'=32] {'grp'}, dimensions={0}, use_global_device_ids=true | all-gather | bytes 1146880 | tf_op jit(solution)/shard_map/all_gather | solution.py:20
  1070.5 1.5 convert_multiply_fusion
  (13 shorter events, 0.1 us)
Async XLA Ops:
  6.5 5.0 copy-start
  6.5 5.0 copy-start.1
  6.5 217.8 %all-gather.11.cloned.1.call-start = ((), (), s32[]{:S(2)}) async-start(), calls=%async_computation.4 | async-start | bytes 2433024 | tf_op jit(solution)/shard_map/all_gather | solution.py:44
  10.8 2.1 copy-start.2
  10.8 393.8 %all-gather.7.cloned.1.call-start = ((), (), s32[]{:S(2)}) async-start(), calls=%async_computation.1 | async-start | bytes 8028160 | tf_op jit(solution)/shard_map/all_gather | solution.py:48
  11.5 952.6 %all-gather.9.cloned.1.call-start = ((), (), s32[]{:S(2)}) async-start(), calls=%async_computation.3 | async-start | bytes 25952256 | tf_op jit(solution)/shard_map/all_gather | solution.py:35
  12.8 1026.5 %reduce-scatter.2.cloned.1.call-start = ((), (), s32[]{:S(2)}) async-start(), calls=%async_computation.2 | async-start | bytes 1146880 | tf_op jit(solution)/shard_map/reduce_scatter | solution.py:17
Sparse Core Ops, SparseCore 0:
  10.9 213.4 all-gather.10
  226.4 178.0 all-gather.6
  406.6 557.5 all-gather.8
  976.4 62.7 reduce-scatter.1
